TPU v7x, 512 devices: a whole 4x4x16 slice. The times are simulated.
512 devices in a mesh: gx: 64 (over x, z), gy: 8 (over y, core).
Axes of the slice: x: 4, y: 4, z: 16, core: 2. Of those that a mesh axis runs over, the one named last changes fastest.
Arguments:
- loads: bfloat16 [64, 8, 512, 128], P('gx', 'gy'), may hold values from -16 to 16
- schur: bfloat16 [64, 8, 512, 512], P('gx', 'gy'), may hold values from -0.5 to 3.5, as said below
- local_inverse: bfloat16 [64, 8, 512, 512], P('gx', 'gy'), may hold values from -0.5 to 3.5, as said below
- coarse_basis: float32 [64, 8, 4, 512], P('gx', 'gy'), may hold values from -0.75 to 0.75
- coarse_inverse: float32 [64, 8, 4, 2048], P('gx', 'gy'), may hold values from -0.5 to 2, as said below
- face_map: int32 [64, 8, 512], P('gx', 'gy'), may hold values from 0 to 511, each once within a row
Outputs:
- solution: float32 [64, 8, 512, 128], P('gx', 'gy')
Inputs may be any that keep to these rules, and one draw needn't show every extreme that they name: `face_map`: each subdomain's row is a permutation of its 512 interface slots. `schur`: each subdomain's matrix is symmetric and positive definite. `local_inverse`: each subdomain's matrix is symmetric and positive definite. `coarse_inverse`: the whole 2048 x 2048 matrix is symmetric and positive definite.
All inputs are finite; a program needn't handle non-finite values.
Results may differ from a plain program's by a relative error of at most 0.0006.
The roundings to bfloat16 on the way count: a program that leaves them out, or rounds other values in their place, can miss the bound.
Values sent between devices are 32-bit elements; how exact they have to be, the bound alone decides.
A program may use at most 64 MiB of HBM per device.

v0:
```python
import jax
import jax.numpy as jnp
from jax import lax
from jax.sharding import PartitionSpec as P

ITERS = 2


def extended(array, sides, width):
    for axis, dim in sides:
        peers, length = (lax.axis_size(axis), array.shape[dim])
        up = [(i, (i + 1) % peers) for i in range(peers - 1)]
        down = [(j, i) for i, j in up]
        last = lax.slice_in_dim(array, length - width, length, axis=dim)
        leading = lax.slice_in_dim(array, 0, width, axis=dim)
        before = lax.ppermute(last, axis, up)
        after = lax.ppermute(leading, axis, down)
        array = jnp.concatenate([before, array, after], axis=dim)
    return array


def face_weights(face_rows):
    index_x = lax.axis_index("gx")
    index_y = lax.axis_index("gy")
    neighbours = [
        index_x > 0,
        index_x < lax.axis_size("gx") - 1,
        index_y > 0,
        index_y < lax.axis_size("gy") - 1,
    ]
    pieces = [
        jnp.broadcast_to(jnp.where(shared, 0.5, 1.0).astype(jnp.float32), (face_rows, 1))
        for shared in neighbours
    ]
    return jnp.concatenate(pieces, axis=0)


def assemble(values):
    face_rows = values.shape[0] // 4
    width_cols = values.shape[1]
    along_x = values[0 : 2 * face_rows].reshape(2, face_rows, width_cols)
    along_y = values[2 * face_rows :].reshape(2, face_rows, width_cols)
    padded_x = extended(along_x, (("gx", 0),), 1)
    padded_y = extended(along_y, (("gy", 0),), 1)
    return jnp.concatenate(
        [
            along_x[0] + padded_x[0],
            along_x[1] + padded_x[3],
            along_y[0] + padded_y[0],
            along_y[1] + padded_y[3],
        ],
        axis=0,
    )


def permuted_product(matrix, halves, face_map, inverse_map):
    local_order = jnp.take(halves, face_map, axis=0)
    product = jnp.dot(matrix, local_order, preferred_element_type=jnp.float32)
    return jnp.take(product, inverse_map, axis=0)


def contract_rows(left_mat, right_mat):
    return lax.dot_general(
        left_mat,
        right_mat,
        (((0,), (0,)), ((), ())),
        precision=lax.Precision.HIGHEST,
        preferred_element_type=jnp.float32,
    )


def times_small(values, small_matrix):
    return jnp.dot(
        values, small_matrix, precision=lax.Precision.HIGHEST, preferred_element_type=jnp.float32
    )


def global_gram(left_mat, right_mat):
    return lax.psum(contract_rows(left_mat, right_mat), ("gx", "gy"))


def solve_gram(matrix, right_side):
    factor = jnp.linalg.cholesky(matrix)
    return jax.scipy.linalg.cho_solve((factor, True), right_side)


def coarse_solve(coarse_input, coarse_rows):
    return jnp.dot(
        coarse_rows,
        lax.all_gather(coarse_input, ("gx", "gy"), axis=0, tiled=True),
        precision=lax.Precision.HIGHEST,
        preferred_element_type=jnp.float32,
    )


def precondition(residual, weights, local_block, basis_block, coarse_rows, face_map, inverse_map):
    scaled = weights * residual
    local_part = permuted_product(local_block, scaled.astype(jnp.bfloat16), face_map, inverse_map)
    coarse_input = jnp.dot(
        basis_block, scaled, precision=lax.Precision.HIGHEST, preferred_element_type=jnp.float32
    )
    coarse_values = coarse_solve(coarse_input, coarse_rows)
    correction = local_part + contract_rows(basis_block, coarse_values)
    update = assemble(weights * correction)
    precond_gram = global_gram(residual, weights * update)
    return (update, precond_gram)


def local(loads, schur, local_inverse, coarse_basis, coarse_inverse, face_map):
    schur_block = schur[0, 0]
    local_block = local_inverse[0, 0]
    basis_block = coarse_basis[0, 0]
    coarse_rows = coarse_inverse[0, 0]
    slot_map = face_map[0, 0]
    unknowns = slot_map.shape[0]
    inverse_map = (
        jnp.zeros((unknowns,), jnp.int32).at[slot_map].set(jnp.arange(unknowns, dtype=jnp.int32))
    )
    weights = face_weights(unknowns // 4)
    residual = assemble(loads[0, 0].astype(jnp.float32))
    solution = jnp.zeros_like(residual)
    update, precond_gram = precondition(
        residual, weights, local_block, basis_block, coarse_rows, slot_map, inverse_map
    )
    direction = update
    for iteration in range(ITERS):
        unassembled = permuted_product(
            schur_block, direction.astype(jnp.bfloat16), slot_map, inverse_map
        )
        image_vec = assemble(unassembled)
        curvature = global_gram(direction, weights * image_vec)
        step_size = solve_gram(curvature, precond_gram)
        solution = solution + times_small(direction, step_size)
        if iteration + 1 < ITERS:
            residual = residual - times_small(image_vec, step_size)
            update, next_gram = precondition(
                residual, weights, local_block, basis_block, coarse_rows, slot_map, inverse_map
            )
            ratio_coef = solve_gram(precond_gram, next_gram)
            direction = update + times_small(direction, ratio_coef)
            precond_gram = next_gram
    return solution[None, None]


def solution(mesh):
    return jax.shard_map(
        local,
        mesh=mesh,
        in_specs=(
            P("gx", "gy", None, None),
            P("gx", "gy", None, None),
            P("gx", "gy", None, None),
            P("gx", "gy", None, None),
            P("gx", "gy", None, None),
            P("gx", "gy", None),
        ),
        out_specs=P("gx", "gy", None, None),
        check_vma=False,
    )
```

profile of v0, /device:TPU:1, one launch (start us, length us, event | category | flops | bytes accessed | tf_op | source)
XLA Modules:
  0.0 1839.8 jit_solution(11037576734090002972)
XLA Ops:
  6.5 1.1 copy.49
  7.7 4.4 collective-permute-start
  12.0 1.3 collective-permute-start.1
  13.3 5.7 collective-permute-start.3
  19.0 1.9 collective-permute-start.2
  21.1 1.1 collective-permute-done.2
  22.3 0.7 copy-done.7
  23.0 0.9 convolution_bitcast_fusion.7
  24.6 2.4 scatter_custom_fusion
  27.3 1.3 gather_fusion
  29.2 1.0 gather_fusion.1
  30.4 167.6 %all-gather.5.cloned.1.call-done = f32[512,4,128]{2,1,0:T(4,128)} async-done(((f32[1,4,128]{2,1,0:T(4,128)}), f32[512,4,128]{2,1,0:T(4,128)}) %all-gather.5.cloned.1.call-update) | async-done | bytes 1048592 | tf_op jit(solution)/shard_map/all_gather | solution.py:90
  197.9 1.9 fusion.62
  200.3 3.1 collective-permute-start.4
  203.4 1.3 collective-permute-done.4
  204.7 1.3 collective-permute-start.5
  206.0 3.0 collective-permute-start.7
  209.1 3.0 collective-permute-start.6
  212.1 1.3 collective-permute-done.6
  213.6 1.3 gather_fusion.2
  215.5 1.0 gather_fusion.3
  216.7 4.6 collective-permute-start.8
  221.4 1.3 collective-permute-done.8
  222.7 1.3 collective-permute-start.9
  224.0 1.9 collective-permute-start.11
  225.9 5.1 collective-permute-start.10
  231.1 1.0 fusion.18
  232.4 1.0 fusion.20
  233.7 458.7 %all-reduce.9.cloned.1.call-done = (f32[128,128]{0,1:T(8,128)}, f32[128,128]{0,1:T(8,128)}) async-done(((f32[128,128]{0,1:T(8,128)}, f32[128,128]{0,1:T(8,128)}), (f32[128,128]{0,1:T(8,128)}, f32[128,128]{0,1:T(8,128)})) %all-reduce.9.cloned.1.call-update) | async-done | bytes 131088 | tf_op jit(solution)/shard_map/psum | solution.py:79
  692.4 1.0 copy.57
  693.5 0.7 copy-done.5
  694.3 11.7 cholesky.59
  707.3 9.8 custom-call.9
  718.1 0.9 convolution_bitcast_fusion.6
  719.3 11.7 cholesky.70
  731.1 1.3 gather_fusion.4
  733.0 1.0 gather_fusion.5
  734.2 143.8 %all-gather.7.cloned.1.call-done = f32[512,4,128]{2,1,0:T(4,128)} async-done(((f32[1,4,128]{2,1,0:T(4,128)}), f32[512,4,128]{2,1,0:T(4,128)}) %all-gather.7.cloned.1.call-update) | async-done | bytes 1048592 | tf_op jit(solution)/shard_map/all_gather | solution.py:90
  878.0 1.9 fusion.60
  880.3 3.1 collective-permute-start.12
  883.4 1.3 collective-permute-done.12
  884.7 1.3 collective-permute-start.13
  886.0 3.0 collective-permute-start.15
  889.1 3.0 collective-permute-start.14
  892.1 0.7 compare_reduce_fusion.1
  893.5 1.0 fusion.16
  895.2 9.8 custom-call.10
  905.0 437.4 %all-reduce.5.cloned.1.call-done = f32[128,128]{1,0:T(8,128)} async-done(((f32[128,128]{1,0:T(8,128)}), f32[128,128]{1,0:T(8,128)}) %all-reduce.5.cloned.1.call-update) | async-done | bytes 65552 | tf_op jit(solution)/shard_map/psum | solution.py:79
  1342.4 1.1 fusion.48
  1344.3 1.3 gather_fusion.6
  1346.2 1.0 gather_fusion.7
  1347.4 3.3 collective-permute-start.16
  1350.7 1.3 collective-permute-done.16
  1352.1 1.3 collective-permute-start.17
  1353.4 1.9 collective-permute-start.19
  1355.3 3.9 collective-permute-start.18
  1359.2 1.0 collective-permute-done.18
  1360.3 1.0 fusion.9
  1361.3 445.5 %all-reduce.7.cloned.1.call-done = f32[128,128]{0,1:T(8,128)} async-done(((f32[128,128]{0,1:T(8,128)}), f32[128,128]{0,1:T(8,128)}) %all-reduce.7.cloned.1.call-update) | async-done | bytes 65552 | tf_op jit(solution)/shard_map/psum | solution.py:79
  1806.9 1.0 copy.69
  1807.9 11.7 cholesky.81
  1820.3 0.7 fusion.40
  1821.0 9.8 custom-call.11
  1831.9 1.3 fusion
  (111 shorter events, 12.3 us)
Async XLA Ops:
  6.5 22.1 %copy-start = (bf16[1,1,512,512]{3,2,1,0:T(8,128)(2,1)S(1)}, bf16[1,1,512,512]{3,2,1,0:T(8,128)(2,1)}, u32[]{:S(2)}) copy-start(bf16[1,1,512,512]{3,2,1,0:T(8,128)(2,1)} %param.15) | copy-start | bytes 1572868
  6.5 191.4 %all-gather.5.cloned.1.call-start = ((), (), s32[]{:S(2)}) async-start(), calls=%async_computation.2 | async-start | bytes 1050624 | tf_op jit(solution)/shard_map/all_gather | solution.py:90
  7.7 13.4 collective-permute-start
  12.0 9.1 collective-permute-start.1
  13.3 7.8 collective-permute-start.3
  19.0 3.2 collective-permute-start.2
  22.3 0.7 copy-start.7
  23.9 0.7 copy-start.8
  23.9 668.5 %all-reduce.9.cloned.1.call-start = ((), (), s32[]{:S(2)}) async-start(), calls=%async_computation.4 | async-start | bytes 262144 | tf_op jit(solution)/shard_map/psum | solution.py:79
  30.2 167.7 %copy-start.6 = (f32[1,1,4,2048]{3,2,1,0:T(4,128)S(1)}, f32[1,1,4,2048]{3,2,1,0:T(4,128)}, u32[]{:S(2)}) copy-start(f32[1,1,4,2048]{3,2,1,0:T(4,128)} %param.17) | copy-start | bytes 98308
  200.3 4.4 collective-permute-start.4
  204.7 7.4 collective-permute-start.5
  206.0 6.1 collective-permute-start.7
  209.1 4.3 collective-permute-start.6
  213.6 1.4 copy-start.1
  216.7 6.0 collective-permute-start.8
  222.7 9.4 collective-permute-start.9
  224.0 8.1 collective-permute-start.11
  225.9 6.4 collective-permute-start.10
  233.4 644.5 %all-gather.7.cloned.1.call-start = ((), (), s32[]{:S(2)}) async-start(), calls=%async_computation.3 | async-start | bytes 1050624 | tf_op jit(solution)/shard_map/all_gather | solution.py:90
  692.4 1.0 copy-start.2
  693.4 0.8 copy-start.5
  719.0 623.4 %all-reduce.5.cloned.1.call-start = ((), (), s32[]{:S(2)}) async-start(), calls=%async_computation | async-start | bytes 131072 | tf_op jit(solution)/shard_map/psum | solution.py:79
  880.3 4.4 collective-permute-start.12
  884.7 8.0 collective-permute-start.13
  886.0 6.7 collective-permute-start.15
  889.1 4.3 collective-permute-start.14
  894.5 912.4 %all-reduce.7.cloned.1.call-start = ((), (), s32[]{:S(2)}) async-start(), calls=%async_computation.1 | async-start | bytes 131072 | tf_op jit(solution)/shard_map/psum | solution.py:79
  1347.4 4.6 collective-permute-start.16
  1352.1 7.1 collective-permute-start.17
  1353.4 5.9 collective-permute-start.19
  1355.3 5.0 collective-permute-start.18
  1806.9 1.0 copy-start.4
  1820.3 10.5 copy-start.3
Sparse Core Ops, SparseCore 0:
  24.0 173.8 all-gather.4
  233.6 458.8 all-reduce.8
  719.1 158.8 all-gather.6
  894.6 447.7 all-reduce.4
  1361.5 445.3 all-reduce.6
where the time goes:
time: 1840 us
  waiting for transfers between devices  1660 us (90%)
  other arithmetic  69 us (4%)
  starting transfers between devices  58 us (3%)
  local copies, waits for them, and re-layouts  18.7 us (1%)
    psum x3, waiting for transfers between devices, global_gram(): return lax.psum(contract_rows(left_mat, right_mat), ('gx', 'gy'))  1340 us
    all_gather x2, waiting for transfers between devices, coarse_solve(): lax.all_gather(coarse_input, ('gx', 'gy'), axis=0, tiled=True)  311 us
    another operation x9, other arithmetic, solve_gram(): factor = jnp.linalg.cholesky(matrix)  37.2 us
  transfers between devices with their start and end apart: 25, of which 14 were waited for; matrix products, arithmetic and copies ran while one was open for 2% of the time, Pallas kernels for 0%

commit v1 on v0

v1 whole, which is shorter than its diff:
```python
import functools

import jax
import jax.numpy as jnp
from jax import lax
from jax.experimental import pallas as pl
from jax.experimental.pallas import tpu as pltpu
from jax.sharding import PartitionSpec as P

NZ = 16
MESH = pl.DeviceIdType.MESH
F32 = jnp.float32
BF16 = jnp.bfloat16
HI = lax.Precision.HIGHEST


def mm(a, b):
    return jnp.dot(a, b, precision=HI, preferred_element_type=F32)


def mm_tn(a, b):
    return lax.dot_general(
        a, b, (((0,), (0,)), ((), ())), precision=HI, preferred_element_type=F32
    )


def iota(shape, dim):
    return lax.broadcasted_iota(jnp.int32, shape, dim)


def eliminate(a_ref, g_ref):
    blocks = a_ref.shape[0]
    lanes = a_ref.shape[2]
    sub = iota((8, lanes), 0)

    def step(i, carry):
        pa = a_ref[i]
        pg = g_ref[i]
        for k in range(8):
            col = jnp.broadcast_to(pa[:, k : k + 1], pa.shape)
            inv = 1.0 / jnp.broadcast_to(col[k : k + 1, :], pa.shape)
            ta = jnp.broadcast_to(pa[k : k + 1, :], pa.shape) * inv
            tg = jnp.broadcast_to(pg[k : k + 1, :], pa.shape) * inv
            pa = jnp.where(sub == k, ta, pa - col * ta)
            pg = jnp.where(sub == k, tg, pg - col * tg)
        rows_a = [jnp.broadcast_to(pa[k : k + 1, :], pa.shape) for k in range(8)]
        rows_g = [jnp.broadcast_to(pg[k : k + 1, :], pa.shape) for k in range(8)]
        a_ref[i] = pltpu.roll(pa, lanes - 8, 1)
        g_ref[i] = pg
        for other in range(1, blocks):
            j = lax.rem(i + other, blocks)
            va = a_ref[j]
            vg = g_ref[j]
            cols = [jnp.broadcast_to(va[:, k : k + 1], va.shape) for k in range(8)]
            for k in range(8):
                va = va - cols[k] * rows_a[k]
                vg = vg - cols[k] * rows_g[k]
            a_ref[j] = pltpu.roll(va, lanes - 8, 1)
            g_ref[j] = vg
        return carry

    lax.fori_loop(0, blocks, step, 0)


def kernel(
    nx, nz, ny,
    loads_ref, schur_ref, linv_ref, basis_ref, cinv_ref, map_ref,
    out_ref,
    mp, sp, lf, xr, basis8, c8, cs, c2, cinb, zg, ps, pr, wcs, ims, imgs,
    res, sch, loc, dirs, upd,
    s1, r1, z1s, z1r, g1s, g1r,
    s2, r2, z2s, z2r, g2s, g2r,
    ga, gb, gc,
    xsend, xrecv, psend, precv,
):
    ni, cols = loads_ref.shape
    face = ni // 4
    n_plane = nx * ny
    gx = lax.axis_index("gx")
    gy = lax.axis_index("gy")
    x = gx // nz
    z = lax.rem(gx, nz)
    me = x * ny + gy
    n_gx = nx * nz

    def plane_id(q):
        return ((q // ny) * nz + z, lax.rem(q, ny))

    def line_id(k):
        return (x * nz + k, gy)

    exists = [gx > 0, gx < n_gx - 1, gy > 0, gy < ny - 1]
    nbr = [(gx - 1, gy), (gx + 1, gy), (gx, gy - 1), (gx, gy + 1)]
    w = [jnp.where(e, 0.5, 1.0).astype(F32) for e in exists]

    barrier = pltpu.get_barrier_semaphore()

    def greet_line(o, carry):
        k = lax.rem(z + o, nz)
        pl.semaphore_signal(barrier, inc=1, device_id=line_id(k), device_id_type=MESH)
        return carry

    def greet_plane(o, carry):
        q = lax.rem(me + o, n_plane)
        pl.semaphore_signal(barrier, inc=1, device_id=plane_id(q), device_id_type=MESH)
        return carry

    lax.fori_loop(1, nz, greet_line, 0)
    lax.fori_loop(1, n_plane, greet_plane, 0)
    for f in range(2):
        @pl.when(exists[f])
        def _():
            pl.semaphore_signal(barrier, inc=1, device_id=nbr[f], device_id_type=MESH)

    lf[...] = loads_ref[...].astype(F32)
    for f in range(4):
        @pl.when(jnp.logical_not(exists[f]))
        def _():
            for ph in range(4):
                xr[ph, f] = jnp.zeros((face, cols), F32)
    basis8[...] = jnp.zeros(basis8.shape, F32)
    basis8[0:4, :] = basis_ref[...]
    c8[...] = jnp.zeros(c8.shape, F32)
    c8[0:4, :] = cinv_ref[...]
    if nz < 16:
        zg[...] = jnp.zeros(zg.shape, F32)

    width = nz * ny * 4
    slab = jnp.concatenate([c8[:, i * width : (i + 1) * width] for i in range(nx)], axis=0)
    hi = slab.astype(BF16)
    rest = slab - hi.astype(F32)
    mid = rest.astype(BF16)
    low = (rest - mid.astype(F32)).astype(BF16)
    parts = jnp.concatenate([hi, mid, low], axis=0)
    src = iota((width, 128), 0)
    dst = iota((width, 128), 1)
    src_z, src_y, src_b = src // (ny * 4), lax.rem(src // 4, ny), lax.rem(src, 4)
    want = jnp.where(src_z * 8 + src_b == dst, src_y, -1)
    for q in range(ny):
        pick = jnp.where(want == q, 1.0, 0.0).astype(BF16)
        moved = jnp.dot(parts, pick, preferred_element_type=F32)
        h = 8 * nx
        moved = moved[0:h] + moved[h : 2 * h] + moved[2 * h : 3 * h]
        for i in range(nx):
            cs[i * ny + q] = moved[8 * i : 8 * i + 8]

    onehot = jnp.where(iota((ni, ni), 0) == map_ref[...], 1.0, 0.0).astype(BF16)

    def permuted(matrix):
        right = lax.dot_general(
            matrix, onehot, (((1,), (1,)), ((), ())), preferred_element_type=F32
        ).astype(BF16)
        return jnp.dot(onehot, right, preferred_element_type=F32).astype(BF16)

    mp[...] = permuted(linv_ref[...])
    sp[...] = permuted(schur_ref[...])

    greeted = (nz - 1) + (n_plane - 1) + exists[0].astype(jnp.int32) + exists[1].astype(jnp.int32)
    pl.semaphore_wait(barrier, greeted)

    def face_copy(ph, f, source):
        return pltpu.make_async_remote_copy(
            src_ref=source.at[pl.ds(f * face, face)],
            dst_ref=xr.at[ph, f ^ 1],
            send_sem=xsend.at[ph, f],
            recv_sem=xrecv.at[ph, f ^ 1],
            device_id=nbr[f],
            device_id_type=MESH,
        )

    def face_arrival(ph, f, source):
        return pltpu.make_async_remote_copy(
            src_ref=source.at[pl.ds(f * face, face)],
            dst_ref=xr.at[ph, f],
            send_sem=xsend.at[ph, f],
            recv_sem=xrecv.at[ph, f],
            device_id=nbr[f],
            device_id_type=MESH,
        )

    def faces_start(ph, source):
        for f in range(4):
            @pl.when(exists[f])
            def _():
                face_copy(ph, f, source).start()

    def faces_wait(ph, source):
        for f in range(4):
            @pl.when(exists[f])
            def _():
                face_arrival(ph, f, source).wait_recv()

    def faces_sent(ph, source):
        for f in range(4):
            @pl.when(exists[f])
            def _():
                face_copy(ph, f, source).wait_send()

    def rows(f):
        return slice(f * face, (f + 1) * face)

    def scatter_plane(t, source, target):
        target[me] = source[me]

        def one(o, carry):
            q = lax.rem(me + o, n_plane)
            pltpu.make_async_remote_copy(
                src_ref=source.at[q], dst_ref=target.at[me],
                send_sem=psend.at[t], recv_sem=precv.at[t],
                device_id=plane_id(q), device_id_type=MESH,
            ).start()
            return carry

        lax.fori_loop(1, n_plane, one, 0)

    def spread_plane(t, source, target):
        target[me] = source[...]

        def one(o, carry):
            q = lax.rem(me + o, n_plane)
            pltpu.make_async_remote_copy(
                src_ref=source, dst_ref=target.at[me],
                send_sem=psend.at[t], recv_sem=precv.at[t],
                device_id=plane_id(q), device_id_type=MESH,
            ).start()
            return carry

        lax.fori_loop(1, n_plane, one, 0)

    def spread_line(t, source, target):
        target[z] = source[...]

        def one(o, carry):
            k = lax.rem(z + o, nz)
            pltpu.make_async_remote_copy(
                src_ref=source, dst_ref=target.at[z],
                send_sem=psend.at[t], recv_sem=precv.at[t],
                device_id=line_id(k), device_id_type=MESH,
            ).start()
            return carry

        lax.fori_loop(1, nz, one, 0)

    def arrived(t, target, n):
        part = target.at[pl.ds(0, n - 1)]
        pltpu.make_async_copy(part, part, precv.at[t]).wait()

    def sent(t, target, n):
        part = target.at[pl.ds(0, n - 1)]
        pltpu.make_async_copy(part, part, psend.at[t]).wait()

    def sum_rows(ref):
        return jnp.sum(ref[...], axis=0)

    def coarse_send(it):
        cinb[it] = mm(basis8[...], sch[...])
        spread_line(1 + 2 * it, cinb.at[it], zg.at[it])

    def coarse_turn(it):
        arrived(1 + 2 * it, zg.at[it], nz)
        gathered = zg[it].reshape(zg.shape[1] * 8, cols)
        partial = mm(c2[...].reshape(n_plane * 8, 128), gathered)
        ps[it] = partial.reshape(n_plane, 8, cols)
        scatter_plane(2 + 2 * it, ps.at[it], pr.at[it])

    def coarse_end(it):
        arrived(2 + 2 * it, pr.at[it], n_plane)
        values = sum_rows(pr.at[it])
        loc[...] = loc[...] + mm_tn(basis8[...], values)
        for f in range(4):
            wcs[it, rows(f), :] = w[f] * loc[rows(f), :]

    def reduce_all(t, source, r_ref, zs, zr, gs, gr):
        scatter_plane(t, source, r_ref)
        arrived(t, r_ref, n_plane)
        zs[...] = sum_rows(r_ref)
        spread_line(t + 1, zs, zr)
        arrived(t + 1, zr, nz)
        gs[...] = sum_rows(zr)
        spread_plane(t + 2, gs, gr)
        arrived(t + 2, gr, n_plane)

    def put_gram(target, at, value):
        per = target.shape[1]
        n = 128 // per
        target[at * n : (at + 1) * n] = value.reshape(n, per, 128)

    def get_gram(ref, at):
        n = 128 // ref.shape[1]
        return ref[at * n : (at + 1) * n].reshape(128, 128)

    def to_blocks(v):
        return v.reshape(16, 8, 128)

    faces_start(0, lf)
    scatter_plane(0, cs, c2)

    faces_wait(0, lf)
    for f in range(4):
        res[rows(f), :] = lf[rows(f), :] + xr[0, f]
        sch[rows(f), :] = w[f] * res[rows(f), :]
    coarse_send(0)
    loc[...] = jnp.dot(mp[...], sch[...].astype(BF16), preferred_element_type=F32)
    arrived(0, c2, n_plane)
    coarse_turn(0)
    coarse_end(0)
    faces_start(1, wcs.at[0])
    put_gram(s1, 0, mm_tn(sch[...], loc[...]))
    faces_wait(1, wcs.at[0])
    for f in range(4):
        dirs[rows(f), :] = wcs[0, rows(f), :] + xr[1, f]
    ims[...] = jnp.dot(sp[...], dirs[...].astype(BF16), preferred_element_type=F32)
    faces_start(2, ims)
    put_gram(s1, 1, mm_tn(dirs[...], ims[...]))
    reduce_all(5, s1, r1, z1s, z1r, g1s, g1r)
    faces_wait(2, ims)
    for f in range(4):
        imgs[rows(f), :] = ims[rows(f), :] + xr[2, f]

    gram0 = get_gram(g1r, 0)
    curv = get_gram(g1r, 1)
    ga[...] = to_blocks(0.5 * (curv + curv.T))
    gb[...] = to_blocks(gram0)
    eliminate(ga, gb)
    alpha = gb[...].reshape(128, 128)

    res[...] = res[...] - mm(imgs[...], alpha)
    for f in range(4):
        sch[rows(f), :] = w[f] * res[rows(f), :]
    coarse_send(1)
    loc[...] = jnp.dot(mp[...], sch[...].astype(BF16), preferred_element_type=F32)
    ga[...] = to_blocks(0.5 * (gram0 + gram0.T))
    gc[...] = to_blocks(jnp.where(iota((128, 128), 0) == iota((128, 128), 1), 1.0, 0.0).astype(F32))
    coarse_turn(1)
    eliminate(ga, gc)
    coarse_end(1)
    faces_start(3, wcs.at[1])
    put_gram(s2, 0, mm_tn(sch[...], loc[...]))
    put_gram(s2, 3, jnp.zeros((128, 128), F32))
    faces_wait(3, wcs.at[1])
    for f in range(4):
        upd[rows(f), :] = wcs[1, rows(f), :] + xr[3, f]
    put_gram(s2, 1, mm_tn(upd[...], ims[...]))
    loc[...] = jnp.dot(sp[...], upd[...].astype(BF16), preferred_element_type=F32)
    put_gram(s2, 2, mm_tn(upd[...], loc[...]))
    reduce_all(8, s2, r2, z2s, z2r, g2s, g2r)

    gram1 = get_gram(g2r, 0)
    cross = get_gram(g2r, 1)
    own = get_gram(g2r, 2)
    ratio = mm(gc[...].reshape(128, 128), gram1)
    half_curv = 0.5 * (curv + curv.T)
    side = mm(cross, ratio)
    curv2 = own + side + side.T + mm_tn(ratio, mm(half_curv, ratio))
    ga[...] = to_blocks(0.5 * (curv2 + curv2.T))
    alpha1 = gb[...].reshape(128, 128)
    gb[...] = to_blocks(gram1)
    eliminate(ga, gb)
    step2 = gb[...].reshape(128, 128)
    step1 = alpha1 + mm(ratio, step2)
    out_ref[...] = mm(dirs[...], step1) + mm(upd[...], step2)

    for ph, source in enumerate((lf, wcs.at[0], ims, wcs.at[1])):
        faces_sent(ph, source)
    for it in range(2):
        sent(1 + 2 * it, zg.at[it], nz)
        sent(2 + 2 * it, pr.at[it], n_plane)
    sent(0, c2, n_plane)
    for t, (r_ref, zr, gr) in ((5, (r1, z1r, g1r)), (8, (r2, z2r, g2r))):
        sent(t, r_ref, n_plane)
        sent(t + 1, zr, nz)
        sent(t + 2, gr, n_plane)


def local(nx, nz, ny, loads, schur, local_inverse, coarse_basis, coarse_inverse, face_map):
    ni, cols = loads.shape[2:]
    n_plane = nx * ny
    vm = lambda *shape: pltpu.VMEM(shape, F32)
    face = ni // 4
    p1, p2 = 256 // n_plane, 512 // n_plane
    zslots = max(nz, 16)
    scratch = [
        pltpu.VMEM((ni, ni), BF16), pltpu.VMEM((ni, ni), BF16),
        vm(ni, cols), vm(4, 4, face, cols),
        vm(8, ni), vm(8, coarse_inverse.shape[3]),
        vm(n_plane, 8, 128), vm(n_plane, 8, 128),
        vm(2, 8, cols), vm(2, zslots, 8, cols),
        vm(2, n_plane, 8, cols), vm(2, n_plane, 8, cols),
        vm(2, ni, cols), vm(ni, cols), vm(ni, cols),
        vm(ni, cols), vm(ni, cols), vm(ni, cols), vm(ni, cols), vm(ni, cols),
    ]
    for p in (p1, p2):
        scratch += [
            vm(n_plane, p, cols), vm(n_plane, p, cols),
            vm(p, cols), vm(nz, p, cols),
            vm(p, cols), vm(n_plane, p, cols),
        ]
    scratch += [vm(16, 8, 128)] * 3
    scratch += [
        pltpu.SemaphoreType.DMA((4, 4)), pltpu.SemaphoreType.DMA((4, 4)),
        pltpu.SemaphoreType.DMA((11,)), pltpu.SemaphoreType.DMA((11,)),
    ]
    vmem = pl.BlockSpec(memory_space=pltpu.VMEM)
    out = pl.pallas_call(
        functools.partial(kernel, nx, nz, ny),
        out_shape=jax.ShapeDtypeStruct((ni, cols), F32),
        in_specs=[vmem] * 6,
        out_specs=vmem,
        scratch_shapes=scratch,
        compiler_params=pltpu.CompilerParams(
            collective_id=0, has_side_effects=True, vmem_limit_bytes=48 * 1024 * 1024
        ),
        name="bddc",
    )(
        loads[0, 0], schur[0, 0], local_inverse[0, 0], coarse_basis[0, 0],
        coarse_inverse[0, 0], face_map[0],
    )
    return out[None, None]


def solution(mesh):
    n_gx, ny = mesh.shape["gx"], mesh.shape["gy"]
    return jax.shard_map(
        functools.partial(local, n_gx // NZ, NZ, ny),
        mesh=mesh,
        in_specs=(
            P("gx", "gy", None, None),
            P("gx", "gy", None, None),
            P("gx", "gy", None, None),
            P("gx", "gy", None, None),
            P("gx", "gy", None, None),
            P("gx", "gy", None),
        ),
        out_specs=P("gx", "gy", None, None),
        check_vma=False,
    )
```

time: 1840 us -> 254 us (0.14)
  waiting for transfers between devices: 1660 us -> 0 us
  Pallas kernels: 0 us -> 249 us
  other arithmetic: 69 us -> 0 us
  starting transfers between devices: 58 us -> 0 us
    psum x3 -> x0, waiting for transfers between devices: 1340 us -> none  [global_gram(): return lax.psum(contract_rows(left_mat, right_mat), ('gx', 'gy'))]
    all_gather x2 -> x0, waiting for transfers between devices: 311 us -> none  [coarse_solve(): lax.all_gather(coarse_input, ('gx', 'gy'), axis=0, tiled=True)]
    pallas_call x0 -> x1, Pallas kernels: none -> 249 us  [local(): pl.pallas_call(functools.partial(kernel, nx, nz, ny), out_shape=jax.Shape...]
    another operation x15 -> x0, other arithmetic: 68.6 us -> none  [the longest x9 37.2 us: solve_gram(): factor = jnp.linalg.cholesky(matrix)]
    ppermute x20 -> x0, starting transfers between devices: 57.5 us -> none  [the longest x10 35.4 us: extended(): before = lax.ppermute(last, axis, up)]
  transfers between devices with their start and end apart: 25 -> 0, of which waited for: 14 -> 0; matrix products, arithmetic and copies ran while one was open for 2% -> 0% of each run, Pallas kernels for 0% -> 0%
where the time goes in v1:
time: 254 us
  Pallas kernels  249 us (98%)
  local copies, waits for them, and re-layouts  5.15 us (2%)
    pallas_call x1, Pallas kernels, local(): pl.pallas_call(functools.partial(kernel, nx, nz, ny), out_shape=jax.Shape...  249 us
    unnamed x13, local copies, waits for them, and re-layouts  5.15 us

profile of v1, /device:TPU:1, one launch (start us, length us, event | category | flops | bytes accessed | tf_op | source)
XLA Modules:
  0.0 254.1 jit_solution(17825945283657168100)
XLA Ops:
  0.0 0.0 copy-start.4
  0.0 0.0 copy-start.5
  0.0 0.7 copy-done.4
  0.7 0.0 copy-done.5
  0.7 0.0 copy-start
  0.7 1.0 copy-done
  1.7 0.0 copy-start.1
  1.7 1.0 copy-done.1
  2.8 0.0 copy-start.2
  2.8 0.9 copy-done.2
  3.7 0.0 copy-start.3
  3.7 0.8 copy-done.3
  4.4 249.0 %bddc.1 = f32[512,128]{1,0:T(8,128)S(1)} custom-call(bf16[512,128]{1,0:T(8,128)(2,1)S(1)} %bitcast.10, bf16[512,512]{1,0:T(8,128)(2,1)S(1)} %bitcast.8, bf16[512,512]{1,0:T(8,128)(2,1)S(1)} %bitcast.9, f32[4,512]{1,0:T(4,128)S(1)} %bitcast.12, f32[4,2048]{1,0:T(4,128)S(1)} %bitcast.11, s32[1,512]{1,0:T(1,128)S(1)} %bitcast.13), custom_call_target="tpu_custom_call" | custom-call | tf_op jit(solution)/shard_map/bddc/pallas_call | solution.py:404
  253.4 0.7 copy.8
Async XLA Ops:
  0.0 0.7 copy-start.4
  0.0 0.7 copy-start.5
  0.7 1.0 copy-start
  1.7 1.0 copy-start.1
  2.8 0.9 copy-start.2
  3.7 0.8 copy-start.3

commit v2 on v1

--- a/solution.py
+++ b/solution.py
@@ -28,49 +28,77 @@
     return lax.broadcasted_iota(jnp.int32, shape, dim)
 
 
-def eliminate(a_ref, g_ref):
-    blocks = a_ref.shape[0]
-    lanes = a_ref.shape[2]
-    sub = iota((8, lanes), 0)
+def split3(v):
+    hi = v.astype(BF16)
+    rest = v - hi.astype(F32)
+    mid = rest.astype(BF16)
+    return hi, mid, (rest - mid.astype(F32)).astype(BF16)
+
+
+def fill_lanes(big):
+    spot = iota(big.shape, 0) - 128 == iota(big.shape, 1) // 128
+    big[...] = jnp.where(spot, 1.0, 0.0).astype(BF16)
+
+
+def eliminate(a_ref, g_ref, big, pad):
+    sub = iota((8, 128), 0)
+
+    def row(v, s):
+        return jnp.broadcast_to(v[s : s + 1, :], (8, 128))
+
+    pad[...] = jnp.zeros(pad.shape, F32)
 
     def step(i, carry):
-        pa = a_ref[i]
-        pg = g_ref[i]
-        for k in range(8):
-            col = jnp.broadcast_to(pa[:, k : k + 1], pa.shape)
-            inv = 1.0 / jnp.broadcast_to(col[k : k + 1, :], pa.shape)
-            ta = jnp.broadcast_to(pa[k : k + 1, :], pa.shape) * inv
-            tg = jnp.broadcast_to(pg[k : k + 1, :], pa.shape) * inv
-            pa = jnp.where(sub == k, ta, pa - col * ta)
-            pg = jnp.where(sub == k, tg, pg - col * tg)
-        rows_a = [jnp.broadcast_to(pa[k : k + 1, :], pa.shape) for k in range(8)]
-        rows_g = [jnp.broadcast_to(pg[k : k + 1, :], pa.shape) for k in range(8)]
-        a_ref[i] = pltpu.roll(pa, lanes - 8, 1)
-        g_ref[i] = pg
-        for other in range(1, blocks):
-            j = lax.rem(i + other, blocks)
-            va = a_ref[j]
-            vg = g_ref[j]
-            cols = [jnp.broadcast_to(va[:, k : k + 1], va.shape) for k in range(8)]
-            for k in range(8):
-                va = va - cols[k] * rows_a[k]
-                vg = vg - cols[k] * rows_g[k]
-            a_ref[j] = pltpu.roll(va, lanes - 8, 1)
-            g_ref[j] = vg
+        at = pl.multiple_of(i * 16, 16)
+        here = pl.ds(at, 16)
+        ra = a_ref[here, :]
+        rg = g_ref[here, :]
+        pick = big[pl.ds(pl.multiple_of(128 - at, 16), 128), :]
+        spread = jnp.dot(
+            jnp.concatenate(split3(ra), axis=0), pick, preferred_element_type=F32
+        )
+        spread = spread[0:16] + spread[16:32] + spread[32:48]
+        lanes = [
+            [spread[8 * h : 8 * h + 8, 128 * j : 128 * j + 128] for h in range(2)]
+            for j in range(16)
+        ]
+        sides = [[ra[0:8], ra[8:16]], [rg[0:8], rg[8:16]]]
+        scale = [jnp.ones((8, 128), F32)] * 2
+        for k in range(16):
+            h, s = divmod(k, 8)
+            inv = 1.0 / row(lanes[k][h], s)
+            factor = [lanes[k][0] * inv, lanes[k][1] * inv]
+            factor[h] = jnp.where(sub == s, 0.0, factor[h])
+            scale[h] = jnp.where(sub == s, inv, scale[h])
+            for col in lanes[k + 1 :] + sides:
+                pivot_row = row(col[h], s)
+                for q in range(2):
+                    col[q] = col[q] - factor[q] * pivot_row
+        pa = jnp.concatenate([sides[0][0] * scale[0], sides[0][1] * scale[1]], axis=0)
+        pg = jnp.concatenate([sides[1][0] * scale[0], sides[1][1] * scale[1]], axis=0)
+        pad[here, 0:128] = pa
+        pad[here, 128:256] = pg
+        change = mm(a_ref[...], pad[...])
+        a_ref[...] = a_ref[...] - change[:, 0:128]
+        g_ref[...] = g_ref[...] - change[:, 128:256]
+        a_ref[here, :] = pa
+        g_ref[here, :] = pg
+        pad[here, :] = jnp.zeros((16, 256), F32)
         return carry
 
-    lax.fori_loop(0, blocks, step, 0)
+    lax.fori_loop(0, 8, step, 0)
 
 
 def kernel(
     nx, nz, ny,
-    loads_ref, schur_ref, linv_ref, basis_ref, cinv_ref, map_ref,
+    loads_hbm, schur_hbm, linv_hbm, basis_hbm, cinv_hbm, map_hbm,
     out_ref,
+    loads_ref, schur_ref, linv_ref, basis_ref, cinv_ref, map_ref, insem,
     mp, sp, lf, xr, basis8, c8, cs, c2, cinb, zg, ps, pr, wcs, ims, imgs,
     res, sch, loc, dirs, upd,
     s1, r1, z1s, z1r, g1s, g1r,
     s2, r2, z2s, z2r, g2s, g2r,
-    ga, gb, gc,
+    ga, gb, gc, big, pad,
     xsend, xrecv, psend, precv,
 ):
     ni, cols = loads_ref.shape
@@ -93,6 +121,16 @@
     nbr = [(gx - 1, gy), (gx + 1, gy), (gx, gy - 1), (gx, gy + 1)]
     w = [jnp.where(e, 0.5, 1.0).astype(F32) for e in exists]
 
+    arrivals = [
+        pltpu.make_async_copy(source, target, insem.at[i])
+        for i, (source, target) in enumerate((
+            (loads_hbm, loads_ref), (cinv_hbm, cinv_ref), (basis_hbm, basis_ref),
+            (map_hbm, map_ref), (linv_hbm, linv_ref), (schur_hbm, schur_ref),
+        ))
+    ]
+    for copy in arrivals:
+        copy.start()
+
     barrier = pltpu.get_barrier_semaphore()
 
     def greet_line(o, carry):
@@ -112,6 +150,9 @@
         def _():
             pl.semaphore_signal(barrier, inc=1, device_id=nbr[f], device_id_type=MESH)
 
+    fill_lanes(big)
+    for copy in arrivals[:4]:
+        copy.wait()
     lf[...] = loads_ref[...].astype(F32)
     for f in range(4):
         @pl.when(jnp.logical_not(exists[f]))
@@ -127,11 +168,7 @@
 
     width = nz * ny * 4
     slab = jnp.concatenate([c8[:, i * width : (i + 1) * width] for i in range(nx)], axis=0)
-    hi = slab.astype(BF16)
-    rest = slab - hi.astype(F32)
-    mid = rest.astype(BF16)
-    low = (rest - mid.astype(F32)).astype(BF16)
-    parts = jnp.concatenate([hi, mid, low], axis=0)
+    parts = jnp.concatenate(split3(slab), axis=0)
     src = iota((width, 128), 0)
     dst = iota((width, 128), 1)
     src_z, src_y, src_b = src // (ny * 4), lax.rem(src // 4, ny), lax.rem(src, 4)
@@ -152,7 +189,9 @@
         ).astype(BF16)
         return jnp.dot(onehot, right, preferred_element_type=F32).astype(BF16)
 
+    arrivals[4].wait()
     mp[...] = permuted(linv_ref[...])
+    arrivals[5].wait()
     sp[...] = permuted(schur_ref[...])
 
     greeted = (nz - 1) + (n_plane - 1) + exists[0].astype(jnp.int32) + exists[1].astype(jnp.int32)
@@ -288,9 +327,6 @@
     def get_gram(ref, at):
         n = 128 // ref.shape[1]
         return ref[at * n : (at + 1) * n].reshape(128, 128)
-
-    def to_blocks(v):
-        return v.reshape(16, 8, 128)
 
     faces_start(0, lf)
     scatter_plane(0, cs, c2)
@@ -319,20 +355,20 @@
 
     gram0 = get_gram(g1r, 0)
     curv = get_gram(g1r, 1)
-    ga[...] = to_blocks(0.5 * (curv + curv.T))
-    gb[...] = to_blocks(gram0)
-    eliminate(ga, gb)
-    alpha = gb[...].reshape(128, 128)
+    ga[...] = 0.5 * (curv + curv.T)
+    gb[...] = gram0
+    eliminate(ga, gb, big, pad)
+    alpha = gb[...]
 
     res[...] = res[...] - mm(imgs[...], alpha)
     for f in range(4):
         sch[rows(f), :] = w[f] * res[rows(f), :]
     coarse_send(1)
     loc[...] = jnp.dot(mp[...], sch[...].astype(BF16), preferred_element_type=F32)
-    ga[...] = to_blocks(0.5 * (gram0 + gram0.T))
-    gc[...] = to_blocks(jnp.where(iota((128, 128), 0) == iota((128, 128), 1), 1.0, 0.0).astype(F32))
+    ga[...] = 0.5 * (gram0 + gram0.T)
+    gc[...] = jnp.where(iota((128, 128), 0) == iota((128, 128), 1), 1.0, 0.0).astype(F32)
+    eliminate(ga, gc, big, pad)
     coarse_turn(1)
-    eliminate(ga, gc)
     coarse_end(1)
     faces_start(3, wcs.at[1])
     put_gram(s2, 0, mm_tn(sch[...], loc[...]))
@@ -348,15 +384,15 @@
     gram1 = get_gram(g2r, 0)
     cross = get_gram(g2r, 1)
     own = get_gram(g2r, 2)
-    ratio = mm(gc[...].reshape(128, 128), gram1)
+    ratio = mm(gc[...], gram1)
     half_curv = 0.5 * (curv + curv.T)
     side = mm(cross, ratio)
     curv2 = own + side + side.T + mm_tn(ratio, mm(half_curv, ratio))
-    ga[...] = to_blocks(0.5 * (curv2 + curv2.T))
-    alpha1 = gb[...].reshape(128, 128)
-    gb[...] = to_blocks(gram1)
-    eliminate(ga, gb)
-    step2 = gb[...].reshape(128, 128)
+    ga[...] = 0.5 * (curv2 + curv2.T)
+    alpha1 = gb[...]
+    gb[...] = gram1
+    eliminate(ga, gb, big, pad)
+    step2 = gb[...]
     step1 = alpha1 + mm(ratio, step2)
     out_ref[...] = mm(dirs[...], step1) + mm(upd[...], step2)
 
@@ -380,6 +416,9 @@
     p1, p2 = 256 // n_plane, 512 // n_plane
     zslots = max(nz, 16)
     scratch = [
+        pltpu.VMEM((ni, cols), BF16), pltpu.VMEM((ni, ni), BF16), pltpu.VMEM((ni, ni), BF16),
+        vm(4, ni), vm(4, coarse_inverse.shape[3]), pltpu.VMEM((1, ni), jnp.int32),
+        pltpu.SemaphoreType.DMA((6,)),
         pltpu.VMEM((ni, ni), BF16), pltpu.VMEM((ni, ni), BF16),
         vm(ni, cols), vm(4, 4, face, cols),
         vm(8, ni), vm(8, coarse_inverse.shape[3]),
@@ -395,7 +434,7 @@
             vm(p, cols), vm(nz, p, cols),
             vm(p, cols), vm(n_plane, p, cols),
         ]
-    scratch += [vm(16, 8, 128)] * 3
+    scratch += [vm(128, 128)] * 3 + [pltpu.VMEM((256, 2048), BF16), vm(128, 256)]
     scratch += [
         pltpu.SemaphoreType.DMA((4, 4)), pltpu.SemaphoreType.DMA((4, 4)),
         pltpu.SemaphoreType.DMA((11,)), pltpu.SemaphoreType.DMA((11,)),
@@ -404,11 +443,11 @@
     out = pl.pallas_call(
         functools.partial(kernel, nx, nz, ny),
         out_shape=jax.ShapeDtypeStruct((ni, cols), F32),
-        in_specs=[vmem] * 6,
+        in_specs=[pl.BlockSpec(memory_space=pltpu.HBM)] * 6,
         out_specs=vmem,
         scratch_shapes=scratch,
         compiler_params=pltpu.CompilerParams(
-            collective_id=0, has_side_effects=True, vmem_limit_bytes=48 * 1024 * 1024
+            collective_id=0, has_side_effects=True, vmem_limit_bytes=67_000_000
         ),
         name="bddc",
     )(

time: 254 us -> 115 us (0.45)
  Pallas kernels: 249 us -> 113 us
  local copies, waits for them, and re-layouts: 5.15 us -> 1.67 us
    pallas_call x1, Pallas kernels: 249 us -> 113 us  [local(): pl.pallas_call(functools.partial(kernel, nx, nz, ny), out_shape=jax.Shape...]
    unnamed x13 -> x1, local copies, waits for them, and re-layouts: 5.15 us -> 1.67 us
where the time goes in v2:
time: 115 us; the launch traced here: 114 us
  Pallas kernels  113 us (98%)
  local copies, waits for them, and re-layouts  1.67 us (1%)
    pallas_call x1, Pallas kernels, local(): pl.pallas_call(functools.partial(kernel, nx, nz, ny), out_shape=jax.Shape...  113 us

profile of v2, /device:TPU:1, one launch (start us, length us, event | category | flops | bytes accessed | tf_op | source)
XLA Modules:
  0.0 114.4 jit_solution(6500980433567309532)
XLA Ops:
  0.0 112.7 %bddc.1 = f32[512,128]{1,0:T(8,128)} custom-call(bf16[512,128]{1,0:T(8,128)(2,1)} %bitcast.10, bf16[512,512]{1,0:T(8,128)(2,1)} %bitcast.8, bf16[512,512]{1,0:T(8,128)(2,1)} %bitcast.9, f32[4,512]{1,0:T(4,128)} %bitcast.12, f32[4,2048]{1,0:T(4,128)} %bitcast.11, s32[1,512]{1,0:T(1,128)} %bitcast.13), custom_call_target="tpu_custom_call" | custom-call | tf_op jit(solution)/shard_map/bddc/pallas_call | solution.py:443
  112.7 1.7 %copy.8 = f32[1,1,512,128]{3,2,1,0:T(8,128)} copy(f32[1,1,512,128]{3,2,1,0:T(8,128)} %bitcast.7) | data formatting | bytes 524288

commit v3 on v2

--- a/solution.py
+++ b/solution.py
@@ -96,9 +96,8 @@
     loads_ref, schur_ref, linv_ref, basis_ref, cinv_ref, map_ref, insem,
     mp, sp, lf, xr, basis8, c8, cs, c2, cinb, zg, ps, pr, wcs, ims, imgs,
     res, sch, loc, dirs, upd,
-    s1, r1, z1s, z1r, g1s, g1r,
-    s2, r2, z2s, z2r, g2s, g2r,
-    ga, gb, gc, big, pad,
+    gsrc, gparts, gmine, gline, gtotal, gresult,
+    ga, gb, gc, gd, ge, cval, big, pad,
     xsend, xrecv, psend, precv,
 ):
     ni, cols = loads_ref.shape
@@ -110,6 +109,7 @@
     z = lax.rem(gx, nz)
     me = x * ny + gy
     n_gx = nx * nz
+    nyc = ny // 2
 
     def plane_id(q):
         return ((q // ny) * nz + z, lax.rem(q, ny))
@@ -238,55 +238,153 @@
     def rows(f):
         return slice(f * face, (f + 1) * face)
 
+    def wrap(v, n):
+        return lax.rem(v, n)
+
+    core = lax.rem(gy, 2)
+    chip_y = gy // 2
+    ys = [wrap(chip_y + o, nyc) for o in range(nyc)]
+    far_y = [nyc // 2] + [o for o in range(nyc) if o not in (0, nyc // 2)] + [0]
+    far_y = far_y if nyc > 1 else [0]
+
+    def over_plane(send):
+        def one(k, carry):
+            xo = wrap(x + 1 + k, nx)
+            for o in far_y:
+                for d in (1, 0):
+                    send(xo, ys[o], wrap(core + d, 2))
+            return carry
+
+        lax.fori_loop(0, nx - 1, one, 0)
+        for o in far_y:
+            for d in (1, 0):
+                if o or d:
+                    send(x, ys[o], wrap(core + d, 2))
+
+    def over_chips(send):
+        def one(k, carry):
+            xo = wrap(x + 1 + k, nx)
+            for o in far_y:
+                send(xo, ys[o])
+            return carry
+
+        lax.fori_loop(0, nx - 1, one, 0)
+        for o in far_y:
+            if o:
+                send(x, ys[o])
+
+    def over_line(send):
+        send(wrap(z + nz // 2, nz))
+
+        def one(k, carry):
+            d = nz // 2 - 1 - k
+            send(wrap(z + d, nz))
+            send(wrap(z + nz - d, nz))
+            return carry
+
+        lax.fori_loop(0, nz // 2 - 1, one, 0)
+
+    def push(t, source, target, device):
+        pltpu.make_async_remote_copy(
+            src_ref=source, dst_ref=target,
+            send_sem=psend.at[t], recv_sem=precv.at[t],
+            device_id=device, device_id_type=MESH,
+        ).start()
+
     def scatter_plane(t, source, target):
         target[me] = source[me]
 
-        def one(o, carry):
-            q = lax.rem(me + o, n_plane)
-            pltpu.make_async_remote_copy(
-                src_ref=source.at[q], dst_ref=target.at[me],
-                send_sem=psend.at[t], recv_sem=precv.at[t],
-                device_id=plane_id(q), device_id_type=MESH,
-            ).start()
-            return carry
-
-        lax.fori_loop(1, n_plane, one, 0)
-
-    def spread_plane(t, source, target):
-        target[me] = source[...]
-
-        def one(o, carry):
-            q = lax.rem(me + o, n_plane)
-            pltpu.make_async_remote_copy(
-                src_ref=source, dst_ref=target.at[me],
-                send_sem=psend.at[t], recv_sem=precv.at[t],
-                device_id=plane_id(q), device_id_type=MESH,
-            ).start()
-            return carry
-
-        lax.fori_loop(1, n_plane, one, 0)
+        def send(xo, yo, co):
+            q = xo * ny + yo * 2 + co
+            push(t, source.at[q], target.at[me], (xo * nz + z, yo * 2 + co))
+
+        over_plane(send)
 
     def spread_line(t, source, target):
         target[z] = source[...]
-
-        def one(o, carry):
-            k = lax.rem(z + o, nz)
-            pltpu.make_async_remote_copy(
-                src_ref=source, dst_ref=target.at[z],
-                send_sem=psend.at[t], recv_sem=precv.at[t],
-                device_id=line_id(k), device_id_type=MESH,
-            ).start()
-            return carry
-
-        lax.fori_loop(1, nz, one, 0)
+        over_line(lambda k: push(t, source, target.at[z], (x * nz + k, gy)))
 
     def arrived(t, target, n):
-        part = target.at[pl.ds(0, n - 1)]
+        part = target.at[pl.ds(0, n)]
         pltpu.make_async_copy(part, part, precv.at[t]).wait()
 
     def sent(t, target, n):
-        part = target.at[pl.ds(0, n - 1)]
+        part = target.at[pl.ds(0, n)]
         pltpu.make_async_copy(part, part, psend.at[t]).wait()
+
+    n_tiles = n_plane // 2
+    my_tile = x * nyc + chip_y
+
+    class Sum:
+        def __init__(self, r, parity):
+            self.t = 5 + 3 * r
+            self.parity = parity
+            self.src, self.parts = gsrc.at[r], gparts.at[r]
+            self.mine, self.line_parts = gmine.at[r], gline.at[r]
+            self.total, self.result = gtotal.at[r], gresult.at[r]
+            self.owner = core == parity
+
+        def scatter(self, matrix):
+            self.src[...] = matrix.reshape(n_tiles, 128 // n_tiles, 128)
+
+            @pl.when(self.owner)
+            def _():
+                self.parts[me] = self.src[my_tile]
+
+            def send(xo, yo):
+                push(
+                    self.t, self.src.at[xo * nyc + yo], self.parts.at[me],
+                    (xo * nz + z, yo * 2 + self.parity),
+                )
+
+            over_chips(send)
+
+            @pl.when(jnp.logical_not(self.owner))
+            def _():
+                send(x, chip_y)
+
+        def line(self):
+            @pl.when(self.owner)
+            def _():
+                arrived(self.t, self.parts, n_plane - 1)
+                self.mine[...] = sum_rows(self.parts)
+                spread_line(self.t + 1, self.mine, self.line_parts)
+
+        def spread(self):
+            @pl.when(self.owner)
+            def _():
+                arrived(self.t + 1, self.line_parts, nz - 1)
+                self.total[...] = sum_rows(self.line_parts)
+                self.result[my_tile] = self.total[...]
+                over_plane(
+                    lambda xo, yo, co: push(
+                        self.t + 2, self.total, self.result.at[my_tile],
+                        (xo * nz + z, yo * 2 + co),
+                    )
+                )
+
+        def finish(self):
+            @pl.when(self.owner)
+            def _():
+                if n_tiles > 1:
+                    arrived(self.t + 2, self.result, n_tiles - 1)
+
+            @pl.when(jnp.logical_not(self.owner))
+            def _():
+                arrived(self.t + 2, self.result, n_tiles)
+
+            return self.result[...].reshape(128, 128)
+
+        def drain(self):
+            @pl.when(self.owner)
+            def _():
+                sent(self.t, self.parts, n_tiles - 1)
+                sent(self.t + 1, self.line_parts, nz - 1)
+                sent(self.t + 2, self.parts, n_plane - 1)
+
+            @pl.when(jnp.logical_not(self.owner))
+            def _():
+                sent(self.t, self.parts, n_tiles)
 
     def sum_rows(ref):
         return jnp.sum(ref[...], axis=0)
@@ -296,116 +394,110 @@
         spread_line(1 + 2 * it, cinb.at[it], zg.at[it])
 
     def coarse_turn(it):
-        arrived(1 + 2 * it, zg.at[it], nz)
+        arrived(1 + 2 * it, zg.at[it], nz - 1)
         gathered = zg[it].reshape(zg.shape[1] * 8, cols)
         partial = mm(c2[...].reshape(n_plane * 8, 128), gathered)
         ps[it] = partial.reshape(n_plane, 8, cols)
         scatter_plane(2 + 2 * it, ps.at[it], pr.at[it])
 
-    def coarse_end(it):
-        arrived(2 + 2 * it, pr.at[it], n_plane)
-        values = sum_rows(pr.at[it])
+    def coarse_values(it):
+        arrived(2 + 2 * it, pr.at[it], n_plane - 1)
+        return sum_rows(pr.at[it])
+
+    def correct(it, values):
         loc[...] = loc[...] + mm_tn(basis8[...], values)
         for f in range(4):
             wcs[it, rows(f), :] = w[f] * loc[rows(f), :]
-
-    def reduce_all(t, source, r_ref, zs, zr, gs, gr):
-        scatter_plane(t, source, r_ref)
-        arrived(t, r_ref, n_plane)
-        zs[...] = sum_rows(r_ref)
-        spread_line(t + 1, zs, zr)
-        arrived(t + 1, zr, nz)
-        gs[...] = sum_rows(zr)
-        spread_plane(t + 2, gs, gr)
-        arrived(t + 2, gr, n_plane)
-
-    def put_gram(target, at, value):
-        per = target.shape[1]
-        n = 128 // per
-        target[at * n : (at + 1) * n] = value.reshape(n, per, 128)
-
-    def get_gram(ref, at):
-        n = 128 // ref.shape[1]
-        return ref[at * n : (at + 1) * n].reshape(128, 128)
+        faces_start(1 + 2 * it, wcs.at[it])
+
+    def symmetric(v):
+        return 0.5 * (v + v.T)
+
+    first_gram, first_curv = Sum(0, 0), Sum(1, 1)
+    next_gram, cross_gram, own_curv = Sum(2, 0), Sum(3, 1), Sum(4, 0)
 
     faces_start(0, lf)
     scatter_plane(0, cs, c2)
-
     faces_wait(0, lf)
     for f in range(4):
         res[rows(f), :] = lf[rows(f), :] + xr[0, f]
         sch[rows(f), :] = w[f] * res[rows(f), :]
     coarse_send(0)
     loc[...] = jnp.dot(mp[...], sch[...].astype(BF16), preferred_element_type=F32)
-    arrived(0, c2, n_plane)
+    arrived(0, c2, n_plane - 1)
     coarse_turn(0)
-    coarse_end(0)
-    faces_start(1, wcs.at[0])
-    put_gram(s1, 0, mm_tn(sch[...], loc[...]))
+    values0 = coarse_values(0)
+    correct(0, values0)
+    cval[...] = values0
+    first_gram.scatter(mm_tn(sch[...], loc[...]))
     faces_wait(1, wcs.at[0])
     for f in range(4):
         dirs[rows(f), :] = wcs[0, rows(f), :] + xr[1, f]
     ims[...] = jnp.dot(sp[...], dirs[...].astype(BF16), preferred_element_type=F32)
     faces_start(2, ims)
-    put_gram(s1, 1, mm_tn(dirs[...], ims[...]))
-    reduce_all(5, s1, r1, z1s, z1r, g1s, g1r)
+    first_curv.scatter(mm_tn(dirs[...], ims[...]))
+
+    first_gram.line()
     faces_wait(2, ims)
     for f in range(4):
         imgs[rows(f), :] = ims[rows(f), :] + xr[2, f]
-
-    gram0 = get_gram(g1r, 0)
-    curv = get_gram(g1r, 1)
-    ga[...] = 0.5 * (curv + curv.T)
+        sch[rows(f), :] = w[f] * imgs[rows(f), :]
+    coarse_send(1)
+    first_curv.line()
+    first_gram.spread()
+    coarse_turn(1)
+    first_curv.spread()
+    gram0 = first_gram.finish()
     gb[...] = gram0
+    ge[...] = symmetric(gram0)
+    gc[...] = jnp.where(iota((128, 128), 0) == iota((128, 128), 1), 1.0, 0.0).astype(F32)
+    image_values = coarse_values(1)
+    half_curv = symmetric(first_curv.finish())
+    gd[...] = half_curv
+    ga[...] = half_curv
     eliminate(ga, gb, big, pad)
     alpha = gb[...]
 
     res[...] = res[...] - mm(imgs[...], alpha)
     for f in range(4):
         sch[rows(f), :] = w[f] * res[rows(f), :]
-    coarse_send(1)
     loc[...] = jnp.dot(mp[...], sch[...].astype(BF16), preferred_element_type=F32)
-    ga[...] = 0.5 * (gram0 + gram0.T)
-    gc[...] = jnp.where(iota((128, 128), 0) == iota((128, 128), 1), 1.0, 0.0).astype(F32)
-    eliminate(ga, gc, big, pad)
-    coarse_turn(1)
-    coarse_end(1)
-    faces_start(3, wcs.at[1])
-    put_gram(s2, 0, mm_tn(sch[...], loc[...]))
-    put_gram(s2, 3, jnp.zeros((128, 128), F32))
+    correct(1, cval[...] - mm(image_values, alpha))
+    next_gram.scatter(mm_tn(sch[...], loc[...]))
     faces_wait(3, wcs.at[1])
     for f in range(4):
         upd[rows(f), :] = wcs[1, rows(f), :] + xr[3, f]
-    put_gram(s2, 1, mm_tn(upd[...], ims[...]))
+    cross_gram.scatter(mm_tn(upd[...], ims[...]))
     loc[...] = jnp.dot(sp[...], upd[...].astype(BF16), preferred_element_type=F32)
-    put_gram(s2, 2, mm_tn(upd[...], loc[...]))
-    reduce_all(8, s2, r2, z2s, z2r, g2s, g2r)
-
-    gram1 = get_gram(g2r, 0)
-    cross = get_gram(g2r, 1)
-    own = get_gram(g2r, 2)
+    own_curv.scatter(mm_tn(upd[...], loc[...]))
+    next_gram.line()
+    cross_gram.line()
+    own_curv.line()
+    eliminate(ge, gc, big, pad)
+    next_gram.spread()
+    cross_gram.spread()
+    own_curv.spread()
+
+    gram1 = next_gram.finish()
     ratio = mm(gc[...], gram1)
-    half_curv = 0.5 * (curv + curv.T)
-    side = mm(cross, ratio)
-    curv2 = own + side + side.T + mm_tn(ratio, mm(half_curv, ratio))
-    ga[...] = 0.5 * (curv2 + curv2.T)
-    alpha1 = gb[...]
+    known = mm_tn(ratio, mm(gd[...], ratio))
+    step1 = gb[...]
     gb[...] = gram1
+    side = mm(cross_gram.finish(), ratio)
+    ga[...] = symmetric(own_curv.finish() + side + side.T + known)
     eliminate(ga, gb, big, pad)
     step2 = gb[...]
-    step1 = alpha1 + mm(ratio, step2)
+    step1 = step1 + mm(ratio, step2)
     out_ref[...] = mm(dirs[...], step1) + mm(upd[...], step2)
 
     for ph, source in enumerate((lf, wcs.at[0], ims, wcs.at[1])):
         faces_sent(ph, source)
     for it in range(2):
-        sent(1 + 2 * it, zg.at[it], nz)
-        sent(2 + 2 * it, pr.at[it], n_plane)
-    sent(0, c2, n_plane)
-    for t, (r_ref, zr, gr) in ((5, (r1, z1r, g1r)), (8, (r2, z2r, g2r))):
-        sent(t, r_ref, n_plane)
-        sent(t + 1, zr, nz)
-        sent(t + 2, gr, n_plane)
+        sent(1 + 2 * it, zg.at[it], nz - 1)
+        sent(2 + 2 * it, pr.at[it], n_plane - 1)
+    sent(0, c2, n_plane - 1)
+    for item in (first_gram, first_curv, next_gram, cross_gram, own_curv):
+        item.drain()
 
 
 def local(nx, nz, ny, loads, schur, local_inverse, coarse_basis, coarse_inverse, face_map):
@@ -413,7 +505,8 @@
     n_plane = nx * ny
     vm = lambda *shape: pltpu.VMEM(shape, F32)
     face = ni // 4
-    p1, p2 = 256 // n_plane, 512 // n_plane
+    n_tiles = n_plane // 2
+    tile = 128 // n_tiles
     zslots = max(nz, 16)
     scratch = [
         pltpu.VMEM((ni, cols), BF16), pltpu.VMEM((ni, ni), BF16), pltpu.VMEM((ni, ni), BF16),
@@ -428,16 +521,14 @@
         vm(2, ni, cols), vm(ni, cols), vm(ni, cols),
         vm(ni, cols), vm(ni, cols), vm(ni, cols), vm(ni, cols), vm(ni, cols),
     ]
-    for p in (p1, p2):
-        scratch += [
-            vm(n_plane, p, cols), vm(n_plane, p, cols),
-            vm(p, cols), vm(nz, p, cols),
-            vm(p, cols), vm(n_plane, p, cols),
-        ]
-    scratch += [vm(128, 128)] * 3 + [pltpu.VMEM((256, 2048), BF16), vm(128, 256)]
+    scratch += [
+        vm(5, n_tiles, tile, cols), vm(5, n_plane, tile, cols), vm(5, tile, cols),
+        vm(5, nz, tile, cols), vm(5, tile, cols), vm(5, n_tiles, tile, cols),
+    ]
+    scratch += [vm(128, 128)] * 5 + [vm(8, cols), pltpu.VMEM((256, 2048), BF16), vm(128, 256)]
     scratch += [
         pltpu.SemaphoreType.DMA((4, 4)), pltpu.SemaphoreType.DMA((4, 4)),
-        pltpu.SemaphoreType.DMA((11,)), pltpu.SemaphoreType.DMA((11,)),
+        pltpu.SemaphoreType.DMA((20,)), pltpu.SemaphoreType.DMA((20,)),
     ]
     vmem = pl.BlockSpec(memory_space=pltpu.VMEM)
     out = pl.pallas_call(

time: 115 us -> 96.1 us (0.84)
  Pallas kernels: 113 us -> 94.3 us
    pallas_call x1, Pallas kernels: 113 us -> 94.3 us  [local(): pl.pallas_call(functools.partial(kernel, nx, nz, ny), out_shape=jax.Shape...]
where the time goes in v3:
time: 96.1 us; the launch traced here: 96 us
  Pallas kernels  94.3 us (98%)
  local copies, waits for them, and re-layouts  1.67 us (2%)
    pallas_call x1, Pallas kernels, local(): pl.pallas_call(functools.partial(kernel, nx, nz, ny), out_shape=jax.Shape...  94.3 us

profile of v3, /device:TPU:1, one launch (start us, length us, event | category | flops | bytes accessed | tf_op | source)
XLA Modules:
  0.0 96.0 jit_solution(10034040857321960304)
XLA Ops:
  0.0 94.3 %bddc.1 = f32[512,128]{1,0:T(8,128)} custom-call(bf16[512,128]{1,0:T(8,128)(2,1)} %bitcast.10, bf16[512,512]{1,0:T(8,128)(2,1)} %bitcast.8, bf16[512,512]{1,0:T(8,128)(2,1)} %bitcast.9, f32[4,512]{1,0:T(4,128)} %bitcast.12, f32[4,2048]{1,0:T(4,128)} %bitcast.11, s32[1,512]{1,0:T(1,128)} %bitcast.13), custom_call_target="tpu_custom_call" | custom-call | tf_op jit(solution)/shard_map/bddc/pallas_call | solution.py:534
  94.3 1.7 %copy.8 = f32[1,1,512,128]{3,2,1,0:T(8,128)} copy(f32[1,1,512,128]{3,2,1,0:T(8,128)} %bitcast.7) | data formatting | bytes 524288

commit v4 on v3

--- a/solution.py
+++ b/solution.py
@@ -417,12 +417,12 @@
     next_gram, cross_gram, own_curv = Sum(2, 0), Sum(3, 1), Sum(4, 0)
 
     faces_start(0, lf)
-    scatter_plane(0, cs, c2)
     faces_wait(0, lf)
     for f in range(4):
         res[rows(f), :] = lf[rows(f), :] + xr[0, f]
         sch[rows(f), :] = w[f] * res[rows(f), :]
     coarse_send(0)
+    scatter_plane(0, cs, c2)
     loc[...] = jnp.dot(mp[...], sch[...].astype(BF16), preferred_element_type=F32)
     arrived(0, c2, n_plane - 1)
     coarse_turn(0)
@@ -434,28 +434,28 @@
     for f in range(4):
         dirs[rows(f), :] = wcs[0, rows(f), :] + xr[1, f]
     ims[...] = jnp.dot(sp[...], dirs[...].astype(BF16), preferred_element_type=F32)
+    first_curv.scatter(mm_tn(dirs[...], ims[...]))
     faces_start(2, ims)
-    first_curv.scatter(mm_tn(dirs[...], ims[...]))
 
     first_gram.line()
+    first_curv.line()
     faces_wait(2, ims)
     for f in range(4):
         imgs[rows(f), :] = ims[rows(f), :] + xr[2, f]
         sch[rows(f), :] = w[f] * imgs[rows(f), :]
     coarse_send(1)
-    first_curv.line()
     first_gram.spread()
+    first_curv.spread()
     coarse_turn(1)
-    first_curv.spread()
     gram0 = first_gram.finish()
     gb[...] = gram0
     ge[...] = symmetric(gram0)
     gc[...] = jnp.where(iota((128, 128), 0) == iota((128, 128), 1), 1.0, 0.0).astype(F32)
-    image_values = coarse_values(1)
     half_curv = symmetric(first_curv.finish())
     gd[...] = half_curv
     ga[...] = half_curv
     eliminate(ga, gb, big, pad)
+    image_values = coarse_values(1)
     alpha = gb[...]
 
     res[...] = res[...] - mm(imgs[...], alpha)
@@ -464,10 +464,10 @@
     loc[...] = jnp.dot(mp[...], sch[...].astype(BF16), preferred_element_type=F32)
     correct(1, cval[...] - mm(image_values, alpha))
     next_gram.scatter(mm_tn(sch[...], loc[...]))
+    cross_gram.scatter(mm_tn(wcs[1], imgs[...]))
     faces_wait(3, wcs.at[1])
     for f in range(4):
         upd[rows(f), :] = wcs[1, rows(f), :] + xr[3, f]
-    cross_gram.scatter(mm_tn(upd[...], ims[...]))
     loc[...] = jnp.dot(sp[...], upd[...].astype(BF16), preferred_element_type=F32)
     own_curv.scatter(mm_tn(upd[...], loc[...]))
     next_gram.line()

time: 96.1 us -> 92 us (0.957)
  Pallas kernels: 94.3 us -> 90.1 us
    pallas_call x1, Pallas kernels: 94.3 us -> 90.1 us  [local(): pl.pallas_call(functools.partial(kernel, nx, nz, ny), out_shape=jax.Shape...]
where the time goes in v4:
time: 92 us; the launch traced here: 91.8 us
  Pallas kernels  90.1 us (98%)
  local copies, waits for them, and re-layouts  1.67 us (2%)
    pallas_call x1, Pallas kernels, local(): pl.pallas_call(functools.partial(kernel, nx, nz, ny), out_shape=jax.Shape...  90.1 us

profile of v4, /device:TPU:1, one launch (start us, length us, event | category | flops | bytes accessed | tf_op | source)
XLA Modules:
  0.0 91.8 jit_solution(6759353380722061904)
XLA Ops:
  0.0 90.1 %bddc.1 = f32[512,128]{1,0:T(8,128)} custom-call(bf16[512,128]{1,0:T(8,128)(2,1)} %bitcast.10, bf16[512,512]{1,0:T(8,128)(2,1)} %bitcast.8, bf16[512,512]{1,0:T(8,128)(2,1)} %bitcast.9, f32[4,512]{1,0:T(4,128)} %bitcast.12, f32[4,2048]{1,0:T(4,128)} %bitcast.11, s32[1,512]{1,0:T(1,128)} %bitcast.13), custom_call_target="tpu_custom_call" | custom-call | tf_op jit(solution)/shard_map/bddc/pallas_call | solution.py:534
  90.2 1.7 %copy.8 = f32[1,1,512,128]{3,2,1,0:T(8,128)} copy(f32[1,1,512,128]{3,2,1,0:T(8,128)} %bitcast.7) | data formatting | bytes 524288

commit v5 on v4

--- a/solution.py
+++ b/solution.py
@@ -131,6 +131,9 @@
     for copy in arrivals:
         copy.start()
 
+    for target in (zg, pr, c2):
+        target[...] = jnp.zeros(target.shape, F32)
+
     barrier = pltpu.get_barrier_semaphore()
 
     def greet_line(o, carry):
@@ -163,8 +166,6 @@
     basis8[0:4, :] = basis_ref[...]
     c8[...] = jnp.zeros(c8.shape, F32)
     c8[0:4, :] = cinv_ref[...]
-    if nz < 16:
-        zg[...] = jnp.zeros(zg.shape, F32)
 
     width = nz * ny * 4
     slab = jnp.concatenate([c8[:, i * width : (i + 1) * width] for i in range(nx)], axis=0)
@@ -293,26 +294,31 @@
 
     def scatter_plane(t, source, target):
         target[me] = source[me]
+        some = pl.ds(0, 4)
 
         def send(xo, yo, co):
             q = xo * ny + yo * 2 + co
-            push(t, source.at[q], target.at[me], (xo * nz + z, yo * 2 + co))
+            push(t, source.at[q, some], target.at[me, some], (xo * nz + z, yo * 2 + co))
 
         over_plane(send)
 
-    def spread_line(t, source, target):
+    def spread_line(t, source, target, n_rows):
         target[z] = source[...]
-        over_line(lambda k: push(t, source, target.at[z], (x * nz + k, gy)))
-
-    def arrived(t, target, n):
-        part = target.at[pl.ds(0, n)]
+        some = pl.ds(0, n_rows)
+        over_line(
+            lambda k: push(t, source.at[some], target.at[z, some], (x * nz + k, gy))
+        )
+
+    def arrived(t, target, n, n_rows):
+        part = target.at[pl.ds(0, n), pl.ds(0, n_rows)]
         pltpu.make_async_copy(part, part, precv.at[t]).wait()
 
-    def sent(t, target, n):
-        part = target.at[pl.ds(0, n)]
+    def sent(t, target, n, n_rows):
+        part = target.at[pl.ds(0, n), pl.ds(0, n_rows)]
         pltpu.make_async_copy(part, part, psend.at[t]).wait()
 
     n_tiles = n_plane // 2
+    tile = 128 // n_tiles
     my_tile = x * nyc + chip_y
 
     class Sum:
@@ -346,14 +352,14 @@
         def line(self):
             @pl.when(self.owner)
             def _():
-                arrived(self.t, self.parts, n_plane - 1)
+                arrived(self.t, self.parts, n_plane - 1, tile)
                 self.mine[...] = sum_rows(self.parts)
-                spread_line(self.t + 1, self.mine, self.line_parts)
+                spread_line(self.t + 1, self.mine, self.line_parts, tile)
 
         def spread(self):
             @pl.when(self.owner)
             def _():
-                arrived(self.t + 1, self.line_parts, nz - 1)
+                arrived(self.t + 1, self.line_parts, nz - 1, tile)
                 self.total[...] = sum_rows(self.line_parts)
                 self.result[my_tile] = self.total[...]
                 over_plane(
@@ -367,41 +373,41 @@
             @pl.when(self.owner)
             def _():
                 if n_tiles > 1:
-                    arrived(self.t + 2, self.result, n_tiles - 1)
+                    arrived(self.t + 2, self.result, n_tiles - 1, tile)
 
             @pl.when(jnp.logical_not(self.owner))
             def _():
-                arrived(self.t + 2, self.result, n_tiles)
+                arrived(self.t + 2, self.result, n_tiles, tile)
 
             return self.result[...].reshape(128, 128)
 
         def drain(self):
             @pl.when(self.owner)
             def _():
-                sent(self.t, self.parts, n_tiles - 1)
-                sent(self.t + 1, self.line_parts, nz - 1)
-                sent(self.t + 2, self.parts, n_plane - 1)
+                sent(self.t, self.parts, n_tiles - 1, tile)
+                sent(self.t + 1, self.line_parts, nz - 1, tile)
+                sent(self.t + 2, self.parts, n_plane - 1, tile)
 
             @pl.when(jnp.logical_not(self.owner))
             def _():
-                sent(self.t, self.parts, n_tiles)
+                sent(self.t, self.parts, n_tiles, tile)
 
     def sum_rows(ref):
         return jnp.sum(ref[...], axis=0)
 
     def coarse_send(it):
         cinb[it] = mm(basis8[...], sch[...])
-        spread_line(1 + 2 * it, cinb.at[it], zg.at[it])
+        spread_line(1 + 2 * it, cinb.at[it], zg.at[it], 4)
 
     def coarse_turn(it):
-        arrived(1 + 2 * it, zg.at[it], nz - 1)
+        arrived(1 + 2 * it, zg.at[it], nz - 1, 4)
         gathered = zg[it].reshape(zg.shape[1] * 8, cols)
         partial = mm(c2[...].reshape(n_plane * 8, 128), gathered)
         ps[it] = partial.reshape(n_plane, 8, cols)
         scatter_plane(2 + 2 * it, ps.at[it], pr.at[it])
 
     def coarse_values(it):
-        arrived(2 + 2 * it, pr.at[it], n_plane - 1)
+        arrived(2 + 2 * it, pr.at[it], n_plane - 1, 4)
         return sum_rows(pr.at[it])
 
     def correct(it, values):
@@ -424,7 +430,7 @@
     coarse_send(0)
     scatter_plane(0, cs, c2)
     loc[...] = jnp.dot(mp[...], sch[...].astype(BF16), preferred_element_type=F32)
-    arrived(0, c2, n_plane - 1)
+    arrived(0, c2, n_plane - 1, 4)
     coarse_turn(0)
     values0 = coarse_values(0)
     correct(0, values0)
@@ -493,9 +499,9 @@
     for ph, source in enumerate((lf, wcs.at[0], ims, wcs.at[1])):
         faces_sent(ph, source)
     for it in range(2):
-        sent(1 + 2 * it, zg.at[it], nz - 1)
-        sent(2 + 2 * it, pr.at[it], n_plane - 1)
-    sent(0, c2, n_plane - 1)
+        sent(1 + 2 * it, zg.at[it], nz - 1, 4)
+        sent(2 + 2 * it, pr.at[it], n_plane - 1, 4)
+    sent(0, c2, n_plane - 1, 4)
     for item in (first_gram, first_curv, next_gram, cross_gram, own_curv):
         item.drain()
 

time: 92 us -> 91.5 us (level)
  no operation moved by 1% of the time
where the time goes in v5:
time: 91.5 us; the launch traced here: 91.4 us
  Pallas kernels  89.7 us (98%)
  local copies, waits for them, and re-layouts  1.67 us (2%)
    pallas_call x1, Pallas kernels, local(): pl.pallas_call(functools.partial(kernel, nx, nz, ny), out_shape=jax.Shape...  89.7 us

profile of v5, /device:TPU:1, one launch (start us, length us, event | category | flops | bytes accessed | tf_op | source)
XLA Modules:
  0.0 91.4 jit_solution(1086087186584129963)
XLA Ops:
  0.0 89.7 %bddc.1 = f32[512,128]{1,0:T(8,128)} custom-call(bf16[512,128]{1,0:T(8,128)(2,1)} %bitcast.10, bf16[512,512]{1,0:T(8,128)(2,1)} %bitcast.8, bf16[512,512]{1,0:T(8,128)(2,1)} %bitcast.9, f32[4,512]{1,0:T(4,128)} %bitcast.12, f32[4,2048]{1,0:T(4,128)} %bitcast.11, s32[1,512]{1,0:T(1,128)} %bitcast.13), custom_call_target="tpu_custom_call" | custom-call | tf_op jit(solution)/shard_map/bddc/pallas_call | solution.py:540
  89.7 1.7 %copy.8 = f32[1,1,512,128]{3,2,1,0:T(8,128)} copy(f32[1,1,512,128]{3,2,1,0:T(8,128)} %bitcast.7) | data formatting | bytes 524288
